TPU v7x, 32 devices: a whole 2x2x4 slice. The times are simulated.
32 devices in a mesh: req: 8 (over z, y), tp: 4 (over x, core).
Axes of the slice: x: 2, y: 2, z: 4, core: 2. Of those that a mesh axis runs over, the one named last changes fastest.
Arguments:
- tokens: bfloat16 [16384, 8192], P('req', 'tp'), may hold values from -6 to 6
- base_projection_weight: bfloat16 [8192, 2048], P('tp'), may hold values from -0.0625 to 0.0625
- adapter_down_maps: bfloat16 [128, 8192, 128], P('req', 'tp'), may hold values from -0.0625 to 0.0625
- adapter_up_maps: bfloat16 [128, 64, 2048], P('req', None, 'tp'), may hold values from -0.75 to 0.75
- block_adapter_ids: int32 [128], replicated, may hold values from 0 to 128, as said below
- adapter_storage_entry: int32 [128], replicated, may hold values from 0 to 127, as said below
Outputs:
- key_value: bfloat16 [16384, 2048], P('req', 'tp')
Inputs may be any that keep to these rules, and one draw needn't show every extreme that they name: `block_adapter_ids`: ids are 0 (base model) or 1 to 128. Adapter k is held by req index adapter_storage_entry[k - 1] // 16. Among the 16 blocks of one req index (blocks i * 16 to i * 16 + 15) at most 2 name adapters held by any one req index; in every draw one req index receives exactly 2 blocks, all naming one adapter, from every req index. `adapter_storage_entry`: A permutation: each storage entry holds exactly one adapter.
All inputs are finite; a program needn't handle non-finite values.
Results may differ from a plain program's by a relative error of at most 0.014.
Values may be sent and summed in bfloat16 or wider, within the bound.
A program may use at most 128 MiB of HBM per device.

v0:
```python
import jax
import jax.numpy as jnp
from jax import lax
from jax.sharding import PartitionSpec as P

KEY_WIDTH = 1024
BLOCK = 128
CAP = 2


def per_device(
    tokens,
    base_projection_weight,
    adapter_down_maps,
    adapter_up_maps,
    block_adapter_ids,
    adapter_storage_entry,
):
    req_count = lax.axis_size("req")
    my_req = lax.axis_index("req")
    my_tp = lax.axis_index("tp")
    row_count, feat_count = tokens.shape
    blk_count = row_count // BLOCK
    adapter_count = adapter_down_maps.shape[0]
    rank_width = adapter_up_maps.shape[1]
    column_count = adapter_up_maps.shape[2]
    half_index = my_tp * column_count // KEY_WIDTH
    tok_blocks = tokens.reshape(blk_count, BLOCK, feat_count)
    partial_value = jnp.dot(tokens, base_projection_weight, preferred_element_type=jnp.float32)
    base_sum = lax.psum_scatter(
        partial_value.astype(jnp.bfloat16), "tp", scatter_dimension=1, tiled=True
    ).astype(jnp.float32)
    ids_all = block_adapter_ids.reshape(req_count, blk_count)
    stored = adapter_storage_entry[jnp.maximum(ids_all - 1, 0)]
    owner_all = jnp.where(ids_all > 0, stored // adapter_count, -1)
    local_all = stored % adapter_count
    block_pos = jnp.arange(blk_count, dtype=jnp.int32)
    before = block_pos[None, :] < block_pos[:, None]
    same_owner = owner_all[:, :, None] == owner_all[:, None, :]
    slot_all = jnp.sum(same_owner & before[None], axis=2)
    ids_own = lax.dynamic_index_in_dim(ids_all, my_req, 0, keepdims=False)
    owner_own = lax.dynamic_index_in_dim(owner_all, my_req, 0, keepdims=False)
    slot_own = lax.dynamic_index_in_dim(slot_all, my_req, 0, keepdims=False)
    spot_index = jnp.maximum(owner_own, 0) * CAP + slot_own
    owner_ids = jnp.arange(req_count, dtype=jnp.int32)[:, None, None]
    slot_ids = jnp.arange(CAP, dtype=jnp.int32)[None, :, None]
    incoming = (owner_all[:, None, :] == my_req) & (slot_all[:, None, :] == slot_ids)
    in_valid = jnp.any(incoming, axis=2)
    input_resident = jnp.sum(jnp.where(incoming, local_all[:, None, :], 0), axis=2)
    outgoing = (owner_own[None, None, :] == owner_ids) & (slot_own[None, None, :] == slot_ids)
    out_valid = jnp.any(outgoing, axis=2)
    pick_block = jnp.sum(jnp.where(outgoing, block_pos[None, None, :], 0), axis=2)
    send_rows = jnp.where(
        out_valid[:, :, None, None], tok_blocks[pick_block], jnp.zeros((), tokens.dtype)
    )
    landed_rows = lax.all_to_all(send_rows, "req", split_axis=0, concat_axis=0, tiled=True)
    partial_shrink = jnp.einsum(
        "vhyf,vhfp->vhyp",
        landed_rows,
        adapter_down_maps[input_resident],
        preferred_element_type=jnp.float32,
    )
    down_projected = lax.psum(partial_shrink.astype(jnp.bfloat16), "tp")
    down_projected_half = lax.dynamic_slice_in_dim(
        down_projected, half_index * rank_width, rank_width, 3
    )
    adapter_delta = jnp.einsum(
        "zflj,zfjb->zflb",
        down_projected_half,
        adapter_up_maps[input_resident],
        preferred_element_type=jnp.float32,
    ).astype(jnp.bfloat16)
    adapter_delta = jnp.where(
        in_valid[:, :, None, None], adapter_delta, jnp.zeros((), jnp.bfloat16)
    )
    returned = lax.all_to_all(adapter_delta, "req", split_axis=0, concat_axis=0, tiled=True)
    own_delta = returned.reshape(req_count * CAP, BLOCK, column_count)[spot_index]
    own_delta = jnp.where(ids_own[:, None, None] > 0, own_delta, jnp.zeros((), jnp.bfloat16))
    return (base_sum + own_delta.reshape(row_count, column_count).astype(jnp.float32)).astype(
        jnp.bfloat16
    )


def solution(mesh):
    placed = (P("req", "tp"), P("tp", None), P("req", "tp", None), P("req", None, "tp"), P(), P())
    return jax.shard_map(
        per_device, mesh=mesh, in_specs=placed, out_specs=P("req", "tp"), check_vma=False
    )
```

profile of v0, /device:TPU:0, one launch (start us, length us, event | category | flops | bytes accessed | tf_op | source)
XLA Modules:
  0.0 343.1 jit_solution(5026651904690158362)
XLA Ops:
  6.5 0.0 copy-start
  6.5 0.7 add_maximum_fusion
  7.3 0.7 reshape.232
  8.0 1.6 gather_fusion
  9.6 0.1 reshape.236
  9.7 0.3 convert_reduce_fusion
  10.1 0.1 fusion.1
  10.2 0.2 and_reduce_fusion
  10.4 0.2 select_reduce_fusion
  10.6 0.1 copy.13
  10.6 0.1 reshape.245
  10.7 0.1 copy.12
  10.8 8.1 %gather_fusion.1 = bf16[16,128,2048]{2,1,0:T(8,128)(2,1)} fusion(bf16[16,128,2048]{2,1,0:T(8,128)(2,1)} %bitcast.36, s32[1024]{0:T(1024)S(1)} %pad_clamp_fusion.2), kind=kCustom, calls=%fused_computation.1 | custom fusion | bytes 16777280 | tf_op jit(solution)/shard_map/gather | solution.py:54
  19.0 7.2 %broadcast_select_fusion = bf16[8,2,128,2048]{3,2,1,0:T(8,128)(2,1)} fusion(bf16[8,2,128,2048]{3,2,1,0:T(8,128)(2,1)} %bitcast.35, pred[8,2]{1,0:T(8,128)(4,1)S(1)} %copy.12), kind=kLoop, calls=%fused_computation.5 | loop fusion | flops 4194304 | bytes 16777232 | tf_op jit(solution)/shard_map/jit(_where)/select_n | solution.py:53
  26.2 7.3 %all-to-all-start = ((bf16[8,2,128,2048]{3,2,1,0:T(8,128)(2,1)}), bf16[8,2,128,2048]{3,2,1,0:T(8,128)(2,1)}, u32[]{:S(2)}, u32[]{:S(2)}) async-start(bf16[8,2,128,2048]{3,2,1,0:T(8,128)(2,1)} %broadcast_select_fusion), calls=%async_computation.1 | async-start | bytes 16777216 | tf_op jit(solution)/shard_map/all_to_all | solution.py:56
  33.5 0.0 all-reduce.2.cloned.1.call-start
  33.5 0.1 copy.14
  33.6 0.1 reshape.253
  33.7 8.1 %gather_fusion.2 = bf16[16,2048,128]{2,1,0:T(8,128)(2,1)} fusion(bf16[16,2048,128]{2,1,0:T(8,128)(2,1)} %param.8, s32[1024]{0:T(1024)S(1)} %pad_clamp_fusion.1), kind=kCustom, calls=%fused_computation.2 | custom fusion | bytes 16777280 | tf_op jit(solution)/shard_map/gather | solution.py:60
  41.8 174.8 %all-to-all-done = bf16[8,2,128,2048]{3,2,1,0:T(8,128)(2,1)} async-done(((bf16[8,2,128,2048]{3,2,1,0:T(8,128)(2,1)}), bf16[8,2,128,2048]{3,2,1,0:T(8,128)(2,1)}, u32[]{:S(2)}, u32[]{:S(2)}) %all-to-all-start) | async-done | bytes 8388640 | tf_op jit(solution)/shard_map/all_to_all | solution.py:56
  216.6 9.4 %convolution_convert_fusion.1 = bf16[8,2,128,128]{2,3,1,0:T(8,128)(2,1)} fusion(bf16[8,2,128,2048]{3,2,1,0:T(8,128)(2,1)} %all-to-all-done, bf16[8,2,2048,128]{3,2,1,0:T(8,128)(2,1)} %bitcast.34), kind=kOutput, calls=%fused_computation.10 | convolution fusion | flops 1074003968 | bytes 17301504 | tf_op jit(solution)/shard_map/vhyf,vhfp->vhyp/dot_general | solution.py:57
  226.0 0.0 all-reduce.2.cloned.1.call-update
  226.0 0.0 reduce-scatter.2.cloned.1.call-start
  226.1 23.6 %convolution_convert_fusion = bf16[2048,2048]{1,0:T(8,128)(2,1)} fusion(bf16[2048,2048]{1,0:T(8,128)(2,1)} %param.6, bf16[2048,2048]{1,0:T(8,128)(2,1)} %param.7), kind=kOutput, calls=%fused_computation.6 | convolution fusion | flops 17184063488 | bytes 25165824 | tf_op jit(solution)/shard_map/dot_general | solution.py:29
  249.6 0.0 reduce-scatter.2.cloned.1.call-update
  249.7 0.0 copy-done
  249.7 0.6 gather_fusion.3
  250.3 0.1 fusion.3
  250.5 0.1 copy.11
  250.6 7.8 %all-reduce.2.cloned.1.call-done = bf16[8,2,128,128]{2,3,1,0:T(8,128)(2,1)} async-done(((bf16[8,2,128,128]{2,3,1,0:T(8,128)(2,1)}), bf16[8,2,128,128]{2,3,1,0:T(8,128)(2,1)}) %all-reduce.2.cloned.1.call-update) | async-done | bytes 524304 | tf_op jit(solution)/shard_map/psum | solution.py:63
  258.4 3.1 convert_select_fusion
  261.5 5.5 %all-to-all-start.1 = ((bf16[8,2,128,512]{3,2,1,0:T(8,128)(2,1)}), bf16[8,2,128,512]{3,2,1,0:T(8,128)(2,1)S(1)}, u32[]{:S(2)}, u32[]{:S(2)}) async-start(bf16[8,2,128,512]{3,2,1,0:T(8,128)(2,1)} %convert_select_fusion), calls=%async_computation.2 | async-start | bytes 4194304 | tf_op jit(solution)/shard_map/all_to_all | solution.py:76
  267.1 0.1 broadcast_bitcast_fusion
  267.1 47.2 %all-to-all-done.1 = bf16[8,2,128,512]{3,2,1,0:T(8,128)(2,1)S(1)} async-done(((bf16[8,2,128,512]{3,2,1,0:T(8,128)(2,1)}), bf16[8,2,128,512]{3,2,1,0:T(8,128)(2,1)S(1)}, u32[]{:S(2)}, u32[]{:S(2)}) %all-to-all-start.1) | async-done | bytes 2097184 | tf_op jit(solution)/shard_map/all_to_all | solution.py:76
  314.3 2.0 gather_fusion.4
  316.3 16.4 %reduce-scatter.2.cloned.1.call-done = bf16[2048,512]{1,0:T(8,128)(2,1)} async-done(((bf16[2048,2048]{1,0:T(8,128)(2,1)}), bf16[2048,512]{1,0:T(8,128)(2,1)}) %reduce-scatter.2.cloned.1.call-update) | async-done | bytes 2097168 | tf_op jit(solution)/shard_map/reduce_scatter | solution.py:30
  332.7 3.5 %add_convert_fusion = bf16[2048,512]{1,0:T(8,128)(2,1)} fusion(bf16[2048,512]{1,0:T(8,128)(2,1)} %reduce-scatter.2.cloned.1.call-done, bf16[16,128,512]{2,1,0:T(8,128)(2,1)} %gather_fusion.4, pred[2048]{0:T(1024)(128)(4,1)S(1)} %broadcast_bitcast_fusion), kind=kLoop, calls=%fused_computation.7 | loop fusion | flops 5242880 | bytes 6293504 | tf_op jit(solution)/shard_map/convert_element_type | solution.py:79
  (14 shorter events, 0.1 us)
Async XLA Ops:
  6.5 243.2 %copy-start = (bf16[16,64,512]{2,1,0:T(8,128)(2,1)S(1)}, bf16[16,64,512]{2,1,0:T(8,128)(2,1)}, u32[]{:S(2)}) copy-start(bf16[16,64,512]{2,1,0:T(8,128)(2,1)} %param.9) | copy-start | bytes 3145732
  26.2 190.4 %all-to-all-start = ((bf16[8,2,128,2048]{3,2,1,0:T(8,128)(2,1)}), bf16[8,2,128,2048]{3,2,1,0:T(8,128)(2,1)}, u32[]{:S(2)}, u32[]{:S(2)}) async-start(bf16[8,2,128,2048]{3,2,1,0:T(8,128)(2,1)} %broadcast_select_fusion), calls=%async_computation.1 | async-start | bytes 16777216 | tf_op jit(solution)/shard_map/all_to_all | solution.py:56
  33.5 224.9 %all-reduce.2.cloned.1.call-start = ((), (), s32[]{:S(2)}) async-start(), calls=%async_computation.4 | async-start | bytes 1048576 | tf_op jit(solution)/shard_map/psum | solution.py:63
  226.0 106.7 %reduce-scatter.2.cloned.1.call-start = ((), (), s32[]{:S(2)}) async-start(), calls=%async_computation.3 | async-start | bytes 10485760 | tf_op jit(solution)/shard_map/reduce_scatter | solution.py:30
  261.5 52.8 %all-to-all-start.1 = ((bf16[8,2,128,512]{3,2,1,0:T(8,128)(2,1)}), bf16[8,2,128,512]{3,2,1,0:T(8,128)(2,1)S(1)}, u32[]{:S(2)}, u32[]{:S(2)}) async-start(bf16[8,2,128,512]{3,2,1,0:T(8,128)(2,1)} %convert_select_fusion), calls=%async_computation.2 | async-start | bytes 4194304 | tf_op jit(solution)/shard_map/all_to_all | solution.py:76
Sparse Core Ops, SparseCore 0:
  226.1 32.2 all-reduce.1
  261.0 71.7 reduce-scatter.1
where the time goes:
time: 344 us; the launch traced here: 343 us
  waiting for transfers between devices  246 us (72%)
  matrix products  36 us (10%)
  local copies, waits for them, and re-layouts  21.9 us (6%)
  between operations  13.5 us (4%)
  starting transfers between devices  12.9 us (4%)
  other arithmetic  12.5 us (4%)
    all_to_all x1, waiting for transfers between devices, per_device(): lax.all_to_all(send_rows, 'req', split_axis=0, concat_axis=0, tiled=True)  175 us
    all_to_all x1, waiting for transfers between devices, per_device(): lax.all_to_all(adapter_delta, 'req', split_axis=0, concat_axis=0, tiled=T...  47.2 us
    dot_general x1, matrix products, per_device(): jnp.dot(tokens, base_projection_weight, preferred_element_type=jnp.float32)  23.6 us
    reduce_scatter x1, waiting for transfers between devices, per_device(): lax.psum_scatter(partial_value.astype(jnp.bfloat16), 'tp', scatter_dimens...  16.4 us
    dot_general x1, matrix products, per_device(): jnp.einsum('vhyf,vhfp->vhyp', landed_rows, adapter_down_maps[input_reside...  9.37 us
    gather x1, local copies, waits for them, and re-layouts, per_device(): adapter_down_maps[input_resident]  8.15 us
    gather x1, local copies, waits for them, and re-layouts, per_device(): tok_blocks[pick_block]  8.14 us
    psum x1, waiting for transfers between devices, per_device(): down_projected = lax.psum(partial_shrink.astype(jnp.bfloat16), 'tp')  7.84 us
  transfers between devices with their start and end apart: 4, of which 4 were waited for; matrix products, arithmetic and copies ran while one was open for 11% of the time, Pallas kernels for 0%

commit v1 on v0

--- a/solution.py
+++ b/solution.py
@@ -60,7 +60,8 @@
         adapter_down_maps[input_resident],
         preferred_element_type=jnp.float32,
     )
-    down_projected = lax.psum(partial_shrink.astype(jnp.bfloat16), "tp")
+    frame = partial_shrink.astype(jnp.bfloat16)
+    down_projected = lax.all_gather(frame, "tp").sum(axis=0)
     down_projected_half = lax.dynamic_slice_in_dim(
         down_projected, half_index * rank_width, rank_width, 3
     )

time: 344 us -> 333 us (0.968)
  waiting for transfers between devices: 246 us -> 237 us
    psum x1 -> x0, waiting for transfers between devices: 7.84 us -> none  [per_device(): down_projected = lax.psum(partial_shrink.astype(jnp.bfloat16), 'tp')]
  transfers between devices with their start and end apart: 4 -> 4, of which waited for: 4 -> 3; matrix products, arithmetic and copies ran while one was open for 11% -> 12% of each run, Pallas kernels for 0% -> 0%
where the time goes in v1:
time: 333 us; the launch traced here: 332 us
  waiting for transfers between devices  237 us (71%)
  matrix products  34.5 us (10%)
  local copies, waits for them, and re-layouts  21.9 us (7%)
  other arithmetic  14.5 us (4%)
  between operations  13.6 us (4%)
  starting transfers between devices  11 us (3%)
    all_to_all x1, waiting for transfers between devices, per_device(): lax.all_to_all(send_rows, 'req', split_axis=0, concat_axis=0, tiled=True)  175 us
    all_to_all x1, waiting for transfers between devices, per_device(): lax.all_to_all(adapter_delta, 'req', split_axis=0, concat_axis=0, tiled=T...  48.3 us
    dot_general x1, matrix products, per_device(): jnp.dot(tokens, base_projection_weight, preferred_element_type=jnp.float32)  23.6 us
    reduce_scatter x1, waiting for transfers between devices, per_device(): lax.psum_scatter(partial_value.astype(jnp.bfloat16), 'tp', scatter_dimens...  13.5 us
    dot_general x1, matrix products, per_device(): jnp.einsum('vhyf,vhfp->vhyp', landed_rows, adapter_down_maps[input_reside...  8.9 us
    gather x1, local copies, waits for them, and re-layouts, per_device(): adapter_down_maps[input_resident]  8.15 us
    gather x1, local copies, waits for them, and re-layouts, per_device(): tok_blocks[pick_block]  8.14 us
    all_to_all x1, starting transfers between devices, per_device(): lax.all_to_all(send_rows, 'req', split_axis=0, concat_axis=0, tiled=True)  7.28 us
  transfers between devices with their start and end apart: 4, of which 3 were waited for; matrix products, arithmetic and copies ran while one was open for 12% of the time, Pallas kernels for 0%

profile of v1, /device:TPU:0, one launch (start us, length us, event | category | flops | bytes accessed | tf_op | source)
XLA Modules:
  0.0 332.1 jit_solution(6182144362621266793)
XLA Ops:
  6.5 0.0 copy-start
  6.5 0.7 add_maximum_fusion
  7.3 0.7 reshape.232
  8.0 1.6 gather_fusion
  9.6 0.1 reshape.236
  9.7 0.3 convert_reduce_fusion
  10.1 0.1 fusion.1
  10.2 0.2 and_reduce_fusion
  10.4 0.2 select_reduce_fusion
  10.6 0.1 copy.16
  10.6 0.1 reshape.245
  10.7 0.1 copy.15
  10.8 8.1 %gather_fusion.1 = bf16[16,128,2048]{2,1,0:T(8,128)(2,1)} fusion(bf16[16,128,2048]{2,1,0:T(8,128)(2,1)} %bitcast.37, s32[1024]{0:T(1024)S(1)} %pad_clamp_fusion.2), kind=kCustom, calls=%fused_computation.1 | custom fusion | bytes 16777280 | tf_op jit(solution)/shard_map/gather | solution.py:54
  19.0 7.2 %broadcast_select_fusion = bf16[8,2,128,2048]{3,2,1,0:T(8,128)(2,1)} fusion(bf16[8,2,128,2048]{3,2,1,0:T(8,128)(2,1)} %bitcast.36, pred[8,2]{1,0:T(8,128)(4,1)S(1)} %copy.15), kind=kLoop, calls=%fused_computation.5 | loop fusion | flops 4194304 | bytes 16777232 | tf_op jit(solution)/shard_map/jit(_where)/select_n | solution.py:53
  26.2 7.3 %all-to-all-start = ((bf16[8,2,128,2048]{3,2,1,0:T(8,128)(2,1)}), bf16[8,2,128,2048]{3,2,1,0:T(8,128)(2,1)}, u32[]{:S(2)}, u32[]{:S(2)}) async-start(bf16[8,2,128,2048]{3,2,1,0:T(8,128)(2,1)} %broadcast_select_fusion), calls=%async_computation.1 | async-start | bytes 16777216 | tf_op jit(solution)/shard_map/all_to_all | solution.py:56
  33.5 0.0 all-gather.3.cloned.1.call-start
  33.5 0.1 copy.17
  33.6 0.1 reshape.253
  33.7 8.1 %gather_fusion.2 = bf16[16,2048,128]{2,1,0:T(8,128)(2,1)} fusion(bf16[16,2048,128]{2,1,0:T(8,128)(2,1)} %param.8, s32[1024]{0:T(1024)S(1)} %pad_clamp_fusion.1), kind=kCustom, calls=%fused_computation.2 | custom fusion | bytes 16777280 | tf_op jit(solution)/shard_map/gather | solution.py:60
  41.8 174.8 %all-to-all-done = bf16[8,2,128,2048]{3,2,1,0:T(8,128)(2,1)} async-done(((bf16[8,2,128,2048]{3,2,1,0:T(8,128)(2,1)}), bf16[8,2,128,2048]{3,2,1,0:T(8,128)(2,1)}, u32[]{:S(2)}, u32[]{:S(2)}) %all-to-all-start) | async-done | bytes 8388640 | tf_op jit(solution)/shard_map/all_to_all | solution.py:56
  216.6 8.9 %convolution_convert_fusion.1 = bf16[8,2,128,128]{3,2,1,0:T(8,128)(2,1)} fusion(bf16[8,2,128,2048]{3,2,1,0:T(8,128)(2,1)} %all-to-all-done, bf16[8,2,2048,128]{3,2,1,0:T(8,128)(2,1)} %bitcast.35), kind=kOutput, calls=%fused_computation.10 | convolution fusion | flops 1074003968 | bytes 17301504 | tf_op jit(solution)/shard_map/vhyf,vhfp->vhyp/dot_general | solution.py:57
  225.5 0.0 all-gather.3.cloned.1.call-update
  225.6 0.0 reduce-scatter.2.cloned.1.call-start
  225.6 23.6 %convolution_convert_fusion = bf16[2048,2048]{1,0:T(8,128)(2,1)} fusion(bf16[2048,2048]{1,0:T(8,128)(2,1)} %param.6, bf16[2048,2048]{1,0:T(8,128)(2,1)} %param.7), kind=kOutput, calls=%fused_computation.6 | convolution fusion | flops 17184063488 | bytes 25165824 | tf_op jit(solution)/shard_map/dot_general | solution.py:29
  249.2 0.0 reduce-scatter.2.cloned.1.call-update
  249.2 0.0 copy-done
  249.2 0.6 gather_fusion.3
  249.8 0.1 fusion.3
  250.0 0.1 copy.14
  250.1 0.0 all-gather.3.cloned.1.call-done
  250.1 2.0 reduce_sum.48
  252.1 2.1 convert_select_fusion
  254.2 3.6 %all-to-all-start.1 = ((bf16[8,2,128,512]{3,2,1,0:T(8,128)(2,1)}), bf16[8,2,128,512]{3,2,1,0:T(8,128)(2,1)S(1)}, u32[]{:S(2)}, u32[]{:S(2)}) async-start(bf16[8,2,128,512]{3,2,1,0:T(8,128)(2,1)} %convert_select_fusion), calls=%async_computation.2 | async-start | bytes 4194304 | tf_op jit(solution)/shard_map/all_to_all | solution.py:77
  257.9 0.1 broadcast_bitcast_fusion
  258.0 48.3 %all-to-all-done.1 = bf16[8,2,128,512]{3,2,1,0:T(8,128)(2,1)S(1)} async-done(((bf16[8,2,128,512]{3,2,1,0:T(8,128)(2,1)}), bf16[8,2,128,512]{3,2,1,0:T(8,128)(2,1)S(1)}, u32[]{:S(2)}, u32[]{:S(2)}) %all-to-all-start.1) | async-done | bytes 2097184 | tf_op jit(solution)/shard_map/all_to_all | solution.py:77
  306.3 2.0 gather_fusion.4
  308.2 13.5 %reduce-scatter.2.cloned.1.call-done = bf16[2048,512]{1,0:T(8,128)(2,1)} async-done(((bf16[2048,2048]{1,0:T(8,128)(2,1)}), bf16[2048,512]{1,0:T(8,128)(2,1)}) %reduce-scatter.2.cloned.1.call-update) | async-done | bytes 2097168 | tf_op jit(solution)/shard_map/reduce_scatter | solution.py:30
  321.7 3.5 %add_convert_fusion = bf16[2048,512]{1,0:T(8,128)(2,1)} fusion(bf16[2048,512]{1,0:T(8,128)(2,1)} %reduce-scatter.2.cloned.1.call-done, bf16[16,128,512]{2,1,0:T(8,128)(2,1)} %gather_fusion.4, pred[2048]{0:T(1024)(128)(4,1)S(1)} %broadcast_bitcast_fusion), kind=kLoop, calls=%fused_computation.7 | loop fusion | flops 5242880 | bytes 6293504 | tf_op jit(solution)/shard_map/convert_element_type | solution.py:80
  (14 shorter events, 0.1 us)
Async XLA Ops:
  6.5 242.7 %copy-start = (bf16[16,64,512]{2,1,0:T(8,128)(2,1)S(1)}, bf16[16,64,512]{2,1,0:T(8,128)(2,1)}, u32[]{:S(2)}) copy-start(bf16[16,64,512]{2,1,0:T(8,128)(2,1)} %param.9) | copy-start | bytes 3145732
  26.2 190.4 %all-to-all-start = ((bf16[8,2,128,2048]{3,2,1,0:T(8,128)(2,1)}), bf16[8,2,128,2048]{3,2,1,0:T(8,128)(2,1)}, u32[]{:S(2)}, u32[]{:S(2)}) async-start(bf16[8,2,128,2048]{3,2,1,0:T(8,128)(2,1)} %broadcast_select_fusion), calls=%async_computation.1 | async-start | bytes 16777216 | tf_op jit(solution)/shard_map/all_to_all | solution.py:56
  33.5 216.6 %all-gather.3.cloned.1.call-start = ((), (), s32[]{:S(2)}) async-start(), calls=%async_computation.4 | async-start | bytes 2621440 | tf_op jit(solution)/shard_map/all_gather | solution.py:64
  225.6 96.2 %reduce-scatter.2.cloned.1.call-start = ((), (), s32[]{:S(2)}) async-start(), calls=%async_computation.3 | async-start | bytes 10485760 | tf_op jit(solution)/shard_map/reduce_scatter | solution.py:30
  254.2 52.1 %all-to-all-start.1 = ((bf16[8,2,128,512]{3,2,1,0:T(8,128)(2,1)}), bf16[8,2,128,512]{3,2,1,0:T(8,128)(2,1)S(1)}, u32[]{:S(2)}, u32[]{:S(2)}) async-start(bf16[8,2,128,512]{3,2,1,0:T(8,128)(2,1)} %convert_select_fusion), calls=%async_computation.2 | async-start | bytes 4194304 | tf_op jit(solution)/shard_map/all_to_all | solution.py:77
Sparse Core Ops, SparseCore 0:
  225.7 21.6 all-gather.2
  249.9 71.7 reduce-scatter.1
